TPU v7x, 32 devices: a whole 2x2x4 slice. The times are simulated.
32 devices in a mesh: dp: 8 (over z, y), tensor: 4 (over x, core).
Axes of the slice: x: 2, y: 2, z: 4, core: 2. Of those that a mesh axis runs over, the one named last changes fastest.
Arguments:
- hidden: bfloat16 [128, 4608], P('dp'), may hold values from -6 to 6
- tied_table: bfloat16 [16384, 4608], P(('dp', 'tensor')), may hold values from -0.25 to 0.25
- targets: int32 [128], P('dp'), may hold values from 0 to 16383
- loss_weight: bfloat16 [128], P('dp'), may hold values from 2 to 20
- inputs: int32 [128], P('dp'), may hold values from 0 to 16383
- embed_grad: bfloat16 [128, 4608], P('dp'), may hold values from -0.09375 to 0.09375
Outputs:
- table_grad: bfloat16 [16384, 4608], P(('dp', 'tensor'))
- hidden_grad: float32 [128, 4608], P('dp', 'tensor')
All inputs are finite; a program needn't handle non-finite values.
Results may differ from a plain program's by a relative error of at most 0.0052.
Values may be sent and summed in bfloat16 or wider, within the bound.
A program may use at most 64 MiB of HBM per device.

v0:
```python
import math
import jax
import jax.numpy as jnp
from jax import lax
from jax.sharding import PartitionSpec as P


def squashed(hidden_rows, tied_table):
    logits = lax.dot_general(
        hidden_rows, tied_table, (((1,), (1,)), ((), ())), preferred_element_type=jnp.float32
    )
    return jnp.tanh(logits / 30.0)


def per_device(hidden, tied_table, targets, loss_weight, inputs, embed_grad):
    width = hidden.shape[1]
    vocab_rows = tied_table.shape[0]
    hidden_all, grad_all, target_all, weight_all, input_all = (
        lax.all_gather(hidden, "dp", axis=0, tiled=True),
        lax.all_gather(embed_grad, "dp", axis=0, tiled=True),
        lax.all_gather(targets, "dp", axis=0, tiled=True),
        lax.all_gather(loss_weight, "dp", axis=0, tiled=True),
        lax.all_gather(inputs, "dp", axis=0, tiled=True),
    )
    offset = lax.axis_index(("dp", "tensor")) * vocab_rows
    columns = offset + jnp.arange(vocab_rows)
    squash = squashed(hidden_all, tied_table)
    expo = jnp.exp(30.0 * squash)
    total = lax.psum(jnp.sum(expo, axis=1), ("dp", "tensor"))
    hits = (target_all[:, None] == columns[None, :]).astype(jnp.float32)
    weights = weight_all.astype(jnp.float32)
    dlogit = (weights[:, None] * (expo / total[:, None] - hits) * (1.0 - squash * squash)).astype(
        jnp.bfloat16
    )
    group_rows = lax.psum_scatter(
        jnp.dot(dlogit, tied_table, preferred_element_type=jnp.float32),
        "dp",
        scatter_dimension=0,
        tiled=True,
    )
    hidden_grad = lax.psum_scatter(group_rows, "tensor", scatter_dimension=1, tiled=True)
    head_term = lax.dot_general(
        dlogit, hidden_all, (((0,), (0,)), ((), ())), preferred_element_type=jnp.float32
    )
    onehot = (input_all[None, :] == columns[:, None]).astype(jnp.bfloat16)
    embed_term = jnp.dot(onehot, grad_all, preferred_element_type=jnp.float32)
    table_grad = (head_term + math.sqrt(width) * embed_term).astype(jnp.bfloat16)
    return (table_grad, hidden_grad)


def solution(mesh):
    placed = (P("dp", None), P(("dp", "tensor"), None), P("dp"), P("dp"), P("dp"), P("dp", None))
    return jax.shard_map(
        per_device,
        mesh=mesh,
        in_specs=placed,
        out_specs=(P(("dp", "tensor"), None), P("dp", "tensor")),
        check_vma=False,
    )
```

profile of v0, /device:TPU:0, one launch (start us, length us, event | category | flops | bytes accessed | tf_op | source)
XLA Modules:
  0.0 241.8 jit_solution(12632579317556245795)
XLA Ops:
  7.2 0.0 all-gather.3.cloned.1.call-start
  7.2 0.7 all-gather.3.cloned.1.call-update
  7.9 0.0 reduce-scatter.3.cloned.1.call-start
  8.0 1.2 dynamic-slice
  9.9 0.9 dynamic-update-slice
  10.7 23.2 %all-reduce = bf16[128]{0:T(256)(128)(2,1)S(1)} all-reduce(bf16[128]{0:T(256)(128)(2,1)S(1)} %dynamic-update-slice), channel_id=1, replica_groups=mesh['dp'=8,'tensor'=4] {'dp'}, use_global_device_ids=true, to_apply=%add | all-reduce | flops 128 | bytes 512
  34.0 0.9 dynamic-update-slice.1
  34.8 0.8 dynamic-update-slice.2
  35.7 6.8 %all-reduce.3 = (s32[128]{0:T(128)S(1)}, s32[128]{0:T(128)S(1)}) all-reduce(s32[128]{0:T(128)S(1)} %dynamic-update-slice.1, s32[128]{0:T(128)S(1)} %dynamic-update-slice.2), channel_id=1, replica_groups=mesh['dp'=8,'tensor'=4] {'dp'}, use_global_device_ids=true, to_apply=%add.1 | all-reduce | flops 256 | bytes 2048
  42.5 11.3 %all-gather.3.cloned.1.call-done = bf16[128,4608]{1,0:T(8,128)(2,1)} async-done(((bf16[16,4608]{1,0:T(8,128)(2,1)}), bf16[128,4608]{1,0:T(8,128)(2,1)}) %all-gather.3.cloned.1.call-update) | async-done | bytes 1179664 | tf_op jit(solution)/shard_map/all_gather | solution.py:19
  53.8 4.4 %fusion.1 = (f32[128]{0:T(128)S(1)}, f32[128,512]{1,0:T(8,128)S(1)}) fusion(bf16[128,4608]{1,0:T(8,128)(2,1)} %all-gather.3.cloned.1.call-done, bf16[512,4608]{1,0:T(8,128)(2,1)} %param.7), kind=kOutput, calls=%fused_computation.5 | convolution fusion | flops 604176256 | bytes 6160896 | tf_op jit(solution)/shard_map/dot_general | solution.py:9
  58.3 38.7 %psum.7 = f32[128]{0:T(128)S(1)} all-reduce(f32[128]{0:T(128)S(1)} %get-tuple-element.4), channel_id=1, replica_groups=mesh['dp'=8,'tensor'=4] {'dp','tensor'}, use_global_device_ids=true, to_apply=%region_1.0 | all-reduce | flops 128 | bytes 1024 | tf_op jit(solution)/shard_map/psum | solution.py:29
  96.9 4.7 %fusion.5 = f32[128,4608]{1,0:T(8,128)} fusion(bf16[512,4608]{1,0:T(8,128)(2,1)} %param.7, f32[128,512]{1,0:T(8,128)S(1)} %get-tuple-element.5, s32[512]{0:T(512)S(1)} %iota_add_fusion, f32[128]{0:T(128)S(1)} %psum.7, f32[128]{0:T(128)S(1)} %convert_element_type.13, s32[128]{0:T(128)S(1)} %get-tuple-element.2), kind=kOutput, calls=%fused_computation.10 | convolution fusion | flops 604635136 | bytes 7343616 | tf_op jit(solution)/shard_map/dot_general | solution.py:36
  101.6 0.0 reduce-scatter.3.cloned.1.call-update
  101.7 0.0 all-gather.5.cloned.1.call-start
  101.7 0.7 all-gather.5.cloned.1.call-update
  102.4 0.0 reduce-scatter.5.cloned.1.call-start
  102.5 0.0 copy-done
  102.5 5.2 %fusion.6 = f32[512,4608]{1,0:T(8,128)} fusion(bf16[128,4608]{1,0:T(8,128)(2,1)S(1)} %copy-done, f32[128,512]{1,0:T(8,128)S(1)} %get-tuple-element.5, s32[512]{0:T(512)S(1)} %iota_add_fusion, f32[128]{0:T(128)S(1)} %psum.7, f32[128]{0:T(128)S(1)} %convert_element_type.13, s32[128]{0:T(128)S(1)} %get-tuple-element.2), kind=kOutput, calls=%fused_computation.11 | convolution fusion | flops 604635136 | bytes 10882560 | tf_op jit(solution)/shard_map/dot_general | solution.py:42
  107.6 63.3 %reduce-scatter.3.cloned.1.call-done = f32[16,4608]{1,0:T(8,128)} async-done(((f32[128,4608]{1,0:T(8,128)}), f32[16,4608]{1,0:T(8,128)}) %reduce-scatter.3.cloned.1.call-update) | async-done | bytes 294928 | tf_op jit(solution)/shard_map/reduce_scatter | solution.py:35
  171.0 0.0 reduce-scatter.5.cloned.1.call-update
  171.0 42.3 %all-gather.5.cloned.1.call-done = bf16[128,4608]{1,0:T(8,128)(2,1)} async-done(((bf16[16,4608]{1,0:T(8,128)(2,1)}), bf16[128,4608]{1,0:T(8,128)(2,1)}) %all-gather.5.cloned.1.call-update) | async-done | bytes 1179664 | tf_op jit(solution)/shard_map/all_gather | solution.py:20
  213.3 7.7 %add_convert_fusion = bf16[512,4608]{1,0:T(8,128)(2,1)} fusion(f32[512,4608]{1,0:T(8,128)} %fusion.6, bf16[128,4608]{1,0:T(8,128)(2,1)} %all-gather.5.cloned.1.call-done, s32[128]{0:T(128)S(1)} %get-tuple-element.3, s32[512]{0:T(512)S(1)} %iota_add_fusion), kind=kOutput, calls=%fused_computation | convolution fusion | flops 611123200 | bytes 15337984 | tf_op jit(solution)/shard_map/dot_general | solution.py:46
  220.9 14.3 %reduce-scatter.5.cloned.1.call-done = f32[16,1152]{1,0:T(8,128)} async-done(((f32[16,4608]{1,0:T(8,128)}), f32[16,1152]{1,0:T(8,128)}) %reduce-scatter.5.cloned.1.call-update) | async-done | bytes 73744 | tf_op jit(solution)/shard_map/reduce_scatter | solution.py:41
  (6 shorter events, 0.0 us)
Async XLA Ops:
  7.2 46.7 %all-gather.3.cloned.1.call-start = ((), (), s32[]{:S(2)}) async-start(), calls=%async_computation.2 | async-start | bytes 1327104 | tf_op jit(solution)/shard_map/all_gather | solution.py:19
  7.9 163.1 %reduce-scatter.3.cloned.1.call-start = ((), (), s32[]{:S(2)}) async-start(), calls=%async_computation.4 | async-start | bytes 2654208 | tf_op jit(solution)/shard_map/reduce_scatter | solution.py:35
  96.9 5.5 %copy-start = (bf16[128,4608]{1,0:T(8,128)(2,1)S(1)}, bf16[128,4608]{1,0:T(8,128)(2,1)}, u32[]{:S(2)}) copy-start(bf16[128,4608]{1,0:T(8,128)(2,1)} %all-gather.3.cloned.1.call-done) | copy-start | bytes 3538948
  101.7 111.6 %all-gather.5.cloned.1.call-start = ((), (), s32[]{:S(2)}) async-start(), calls=%async_computation.3 | async-start | bytes 1327104 | tf_op jit(solution)/shard_map/all_gather | solution.py:20
  102.4 132.9 %reduce-scatter.5.cloned.1.call-start = ((), (), s32[]{:S(2)}) async-start(), calls=%async_computation.5 | async-start | bytes 368640 | tf_op jit(solution)/shard_map/reduce_scatter | solution.py:41
Sparse Core Ops, SparseCore 0:
  10.2 43.6 all-gather.2
  101.8 69.1 reduce-scatter.2
  173.1 40.0 all-gather.4
  216.2 19.0 reduce-scatter.4
where the time goes:
time: 242 us
  waiting for transfers between devices  133 us (55%)
  blocking collectives  68.7 us (28%)
  matrix products  22 us (9%)
  between operations  14.5 us (6%)
  local copies, waits for them, and re-layouts  3.81 us (2%)
    reduce_scatter x1, waiting for transfers between devices, per_device(): lax.psum_scatter(jnp.dot(dlogit, tied_table, preferred_element_type=jnp.f...  63.3 us
    all_gather x1, waiting for transfers between devices, per_device(): lax.all_gather(embed_grad, 'dp', axis=0, tiled=True)  42.3 us
    psum x1, blocking collectives, per_device(): total = lax.psum(jnp.sum(expo, axis=1), ('dp', 'tensor'))  38.7 us
    unnamed x2, blocking collectives  30.1 us
    reduce_scatter x1, waiting for transfers between devices, per_device(): lax.psum_scatter(group_rows, 'tensor', scatter_dimension=1, tiled=True)  14.3 us
    all_gather x1, waiting for transfers between devices, per_device(): lax.all_gather(hidden, 'dp', axis=0, tiled=True)  11.3 us
    dot_general x1, matrix products, per_device(): embed_term = jnp.dot(onehot, grad_all, preferred_element_type=jnp.float32)  7.67 us
    dot_general x1, matrix products, per_device(): lax.dot_general(dlogit, hidden_all, (((0,), (0,)), ((), ())), preferred_e...  5.16 us
  transfers between devices with their start and end apart: 4, of which 4 were waited for; matrix products, arithmetic and copies ran while one was open for 7% of the time, Pallas kernels for 0%

commit v1 on v0

--- a/solution.py
+++ b/solution.py
@@ -1,8 +1,28 @@
+import functools
 import math
 import jax
 import jax.numpy as jnp
 from jax import lax
 from jax.sharding import PartitionSpec as P
+
+
+def arrange_flows_all(q_in, ax_name):
+    n_axis = jax.lax.axis_size(ax_name)
+    inbox = tuple(((pp, (pp + 1) % n_axis) for pp in range(n_axis)))
+    y1, res = ([q_in], [q_in])
+    pool = tuple(((pp, (pp - 1) % n_axis) for pp in range(n_axis)))
+    for _ in range(n_axis // 2):
+        block_out = jax.lax.ppermute(y1[-1], ax_name, perm=inbox)
+        y1.append(block_out)
+    for _ in range((n_axis - 1) // 2):
+        outcome_arr = jax.lax.ppermute(res[-1], ax_name, perm=pool)
+        res.append(outcome_arr)
+    vec_out = jnp.concatenate([*y1[::-1], *res[1:]], 0)
+    moved = jax.lax.axis_index(ax_name)
+    return jnp.roll(vec_out, (moved - n_axis // 2) * q_in.shape[0], 0)
+
+
+map_meshes = functools.partial(arrange_flows_all, ax_name="dp")
 
 
 def squashed(hidden_rows, tied_table):
@@ -16,7 +36,7 @@
     width = hidden.shape[1]
     vocab_rows = tied_table.shape[0]
     hidden_all, grad_all, target_all, weight_all, input_all = (
-        lax.all_gather(hidden, "dp", axis=0, tiled=True),
+        map_meshes(hidden),
         lax.all_gather(embed_grad, "dp", axis=0, tiled=True),
         lax.all_gather(targets, "dp", axis=0, tiled=True),
         lax.all_gather(loss_weight, "dp", axis=0, tiled=True),

time: 242 us -> 263 us (1.087)
  starting transfers between devices: 0.16 us -> 17.3 us
  waiting for transfers between devices: 133 us -> 143 us
  matrix products: 22 us -> 12.8 us
    ppermute x0 -> x7, starting transfers between devices: none -> 17.2 us  [the longest x3 13.6 us: arrange_flows_all(): outcome_arr = jax.lax.ppermute(res[-1], ax_name, perm=pool)]
    ppermute x0 -> x7, waiting for transfers between devices: none -> 15 us  [the longest x4 13.3 us: arrange_flows_all(): block_out = jax.lax.ppermute(y1[-1], ax_name, perm=inbox)]
    all_gather x1 -> x0, waiting for transfers between devices: 11.3 us -> none  [per_device(): lax.all_gather(hidden, 'dp', axis=0, tiled=True)]
    reduce_scatter x1, waiting for transfers between devices: 63.3 us -> 68.9 us  [per_device(): lax.psum_scatter(jnp.dot(dlogit, tied_table, preferred_element_type=jnp.f...]
    dot_general x1, matrix products: 7.67 us -> 2.69 us  [per_device(): embed_term = jnp.dot(onehot, grad_all, preferred_element_type=jnp.float32)]
    dot_general x1, matrix products: 4.45 us -> 1.75 us  [squashed(): lax.dot_general(hidden_rows, tied_table, (((1,), (1,)), ((), ())), prefer...]
    unnamed x9 -> x24, local copies, waits for them, and re-layouts: 3.81 us -> 5.8 us
  transfers between devices with their start and end apart: 4 -> 10, of which waited for: 4 -> 7; matrix products, arithmetic and copies ran while one was open for 7% -> 4% of each run, Pallas kernels for 0% -> 0%
where the time goes in v1:
time: 263 us; the launch traced here: 262 us
  waiting for transfers between devices  143 us (54%)
  blocking collectives  69.2 us (26%)
  starting transfers between devices  17.3 us (7%)
  between operations  14.5 us (6%)
  matrix products  12.8 us (5%)
  local copies, waits for them, and re-layouts  5.81 us (2%)
    reduce_scatter x1, waiting for transfers between devices, per_device(): lax.psum_scatter(jnp.dot(dlogit, tied_table, preferred_element_type=jnp.f...  68.9 us
    all_gather x1, waiting for transfers between devices, per_device(): lax.all_gather(embed_grad, 'dp', axis=0, tiled=True)  42.3 us
    psum x1, blocking collectives, per_device(): total = lax.psum(jnp.sum(expo, axis=1), ('dp', 'tensor'))  40.6 us
    unnamed x2, blocking collectives  28.6 us
    reduce_scatter x1, waiting for transfers between devices, per_device(): lax.psum_scatter(group_rows, 'tensor', scatter_dimension=1, tiled=True)  15.7 us
    ppermute x3, starting transfers between devices, arrange_flows_all(): outcome_arr = jax.lax.ppermute(res[-1], ax_name, perm=pool)  13.6 us
    ppermute x4, waiting for transfers between devices, arrange_flows_all(): block_out = jax.lax.ppermute(y1[-1], ax_name, perm=inbox)  13.3 us
    unnamed x24, local copies, waits for them, and re-layouts  5.8 us
  transfers between devices with their start and end apart: 10, of which 7 were waited for; matrix products, arithmetic and copies ran while one was open for 4% of the time, Pallas kernels for 0%

profile of v1, /device:TPU:0, one launch (start us, length us, event | category | flops | bytes accessed | tf_op | source)
XLA Modules:
  0.0 262.2 jit_solution(12004227245258094636)
XLA Ops:
  7.2 3.0 %collective-permute-start = (bf16[16,4608]{1,0:T(8,128)(2,1)}, bf16[16,4608]{1,0:T(8,128)(2,1)S(1)}, u32[]{:S(2)}, u32[]{:S(2)}) collective-permute-start(bf16[16,4608]{1,0:T(8,128)(2,1)} %param.6), channel_id=1, source_target_pairs={{0,4},{4,8},{8,12},{12,16},{16,20},{20,24},{24,28},{28,0},{1,5},{5... | collective-permute-start | bytes 442376 | tf_op jit(solution)/shard_map/ppermute | solution.py:15
  10.2 7.1 %collective-permute-done = bf16[16,4608]{1,0:T(8,128)(2,1)S(1)} collective-permute-done((bf16[16,4608]{1,0:T(8,128)(2,1)}, bf16[16,4608]{1,0:T(8,128)(2,1)S(1)}, u32[]{:S(2)}, u32[]{:S(2)}) %collective-permute-start) | collective-permute-done | bytes 147488 | tf_op jit(solution)/shard_map/ppermute | solution.py:15
  17.3 4.7 %collective-permute-start.4 = (bf16[16,4608]{1,0:T(8,128)(2,1)}, bf16[16,4608]{1,0:T(8,128)(2,1)S(1)}, u32[]{:S(2)}, u32[]{:S(2)}) collective-permute-start(bf16[16,4608]{1,0:T(8,128)(2,1)} %param.6), channel_id=1, source_target_pairs={{0,28},{4,0},{8,4},{12,8},{16,12},{20,16},{24,20},{28,24},{1,29},{... | collective-permute-start | bytes 442376 | tf_op jit(solution)/shard_map/ppermute | solution.py:18
  22.1 3.2 %collective-permute-done.1 = bf16[16,4608]{1,0:T(8,128)(2,1)S(1)} collective-permute-done((bf16[16,4608]{1,0:T(8,128)(2,1)S(1)}, bf16[16,4608]{1,0:T(8,128)(2,1)S(1)}, u32[]{:S(2)}, u32[]{:S(2)}) %collective-permute-start.1) | collective-permute-done | bytes 147488 | tf_op jit(solution)/shard_map/ppermute | solution.py:15
  25.8 4.3 %collective-permute-start.5 = (bf16[16,4608]{1,0:T(8,128)(2,1)S(1)}, bf16[16,4608]{1,0:T(8,128)(2,1)S(1)}, u32[]{:S(2)}, u32[]{:S(2)}) collective-permute-start(bf16[16,4608]{1,0:T(8,128)(2,1)S(1)} %collective-permute-done.4), channel_id=1, source_target_pairs={{0,28},{4,0},{8,4},{12,8},{16,12},{20,16},{24,20},{28,24},{1,29},{... | collective-permute-start | bytes 442376 | tf_op jit(solution)/shard_map/ppermute | solution.py:18
  30.2 3.0 %collective-permute-done.2 = bf16[16,4608]{1,0:T(8,128)(2,1)S(1)} collective-permute-done((bf16[16,4608]{1,0:T(8,128)(2,1)S(1)}, bf16[16,4608]{1,0:T(8,128)(2,1)S(1)}, u32[]{:S(2)}, u32[]{:S(2)}) %collective-permute-start.2) | collective-permute-done | bytes 147488 | tf_op jit(solution)/shard_map/ppermute | solution.py:15
  33.2 1.2 dynamic-slice
  35.1 0.9 dynamic-update-slice
  35.9 21.8 %all-reduce = bf16[128]{0:T(256)(128)(2,1)S(1)} all-reduce(bf16[128]{0:T(256)(128)(2,1)S(1)} %dynamic-update-slice), channel_id=1, replica_groups=mesh['dp'=8,'tensor'=4] {'dp'}, use_global_device_ids=true, to_apply=%add | all-reduce | flops 128 | bytes 512
  57.8 0.9 dynamic-update-slice.2
  58.6 0.8 dynamic-update-slice.1
  59.5 6.8 %all-reduce.3 = (s32[128]{0:T(128)S(1)}, s32[128]{0:T(128)S(1)}) all-reduce(s32[128]{0:T(128)S(1)} %dynamic-update-slice.2, s32[128]{0:T(128)S(1)} %dynamic-update-slice.1), channel_id=1, replica_groups=mesh['dp'=8,'tensor'=4] {'dp'}, use_global_device_ids=true, to_apply=%add.2 | all-reduce | flops 256 | bytes 2048
  66.3 4.6 %collective-permute-start.6 = (bf16[16,4608]{1,0:T(8,128)(2,1)S(1)}, bf16[16,4608]{1,0:T(8,128)(2,1)S(1)}, u32[]{:S(2)}, u32[]{:S(2)}) collective-permute-start(bf16[16,4608]{1,0:T(8,128)(2,1)S(1)} %collective-permute-done.5), channel_id=1, source_target_pairs={{0,28},{4,0},{8,4},{12,8},{16,12},{20,16},{24,20},{28,24},{1,29},{... | collective-permute-start | bytes 442376 | tf_op jit(solution)/shard_map/ppermute | solution.py:18
  70.9 0.9 constant_dynamic-update-slice_fusion.11
  71.9 1.6 collective-permute-done.6
  73.6 0.9 constant_dynamic-update-slice_fusion.3
  74.6 1.7 fusion.3
  76.3 40.6 %psum.7 = f32[128]{0:T(128)S(1)} all-reduce(f32[128]{0:T(128)S(1)} %get-tuple-element.4), channel_id=1, replica_groups=mesh['dp'=8,'tensor'=4] {'dp','tensor'}, use_global_device_ids=true, to_apply=%region_1.2 | all-reduce | flops 128 | bytes 1024 | tf_op jit(solution)/shard_map/psum | solution.py:49
  116.9 4.6 %fusion.10 = f32[128,4608]{1,0:T(8,128)} fusion(bf16[512,4608]{1,0:T(8,128)(2,1)} %param.7, f32[128,512]{1,0:T(8,128)S(1)} %get-tuple-element.5, s32[512]{0:T(512)S(1)} %iota_add_fusion, f32[128]{0:T(128)S(1)} %psum.7, f32[128]{0:T(128)S(1)} %convert_element_type.13, s32[128]{0:T(128)S(1)} %get-tuple-element.3), kind=kOutput, calls=%fused_computation.31 | convolution fusion | flops 604635136 | bytes 7343616 | tf_op jit(solution)/shard_map/dot_general | solution.py:56
  122.3 68.9 %reduce-scatter.3.cloned.1.call-done = f32[16,4608]{1,0:T(8,128)} async-done(((f32[128,4608]{1,0:T(8,128)}), f32[16,4608]{1,0:T(8,128)}) %reduce-scatter.3.cloned.1.call-update) | async-done | bytes 294928 | tf_op jit(solution)/shard_map/reduce_scatter | solution.py:55
  191.3 42.3 %all-gather.2.cloned.1.call-done = bf16[128,4608]{1,0:T(8,128)(2,1)} async-done(((bf16[16,4608]{1,0:T(8,128)(2,1)}), bf16[128,4608]{1,0:T(8,128)(2,1)}) %all-gather.2.cloned.1.call-update) | async-done | bytes 1179664 | tf_op jit(solution)/shard_map/all_gather | solution.py:40
  233.5 2.7 %fusion.4 = f32[512,4608]{1,0:T(8,128)S(1)} fusion(bf16[128,4608]{1,0:T(8,128)(2,1)} %all-gather.2.cloned.1.call-done, s32[128]{0:T(128)S(1)} %get-tuple-element.2, s32[512]{0:T(512)S(1)} %iota_add_fusion), kind=kOutput, calls=%fused_computation.8 | convolution fusion | flops 604045312 | bytes 10619392 | tf_op jit(solution)/shard_map/dot_general | solution.py:66
  236.2 3.7 %add_convert_fusion = bf16[512,4608]{1,0:T(8,128)(2,1)} fusion(f32[512,4608]{1,0:T(8,128)S(1)} %fusion.4, bf16[256,4608]{1,0:T(8,128)(2,1)S(1)} %constant_dynamic-update-slice_fusion, s32[]{:T(128)S(6)} %select_n.14, f32[128,512]{1,0:T(8,128)S(1)} %get-tuple-element.5, s32[512]{0:T(512)S(1)} %iota_add_fusion, f32[128]{0:T(128)S(1)} %psum.7, ...), kind=kOutput, calls=%fused_computation | convolution fusion | flops 611713024 | bytes 15601156 | tf_op jit(solution)/shard_map/dot_general | solution.py:62
  240.0 15.7 %reduce-scatter.5.cloned.1.call-done = f32[16,1152]{1,0:T(8,128)} async-done(((f32[16,4608]{1,0:T(8,128)}), f32[16,1152]{1,0:T(8,128)}) %reduce-scatter.5.cloned.1.call-update) | async-done | bytes 73744 | tf_op jit(solution)/shard_map/reduce_scatter | solution.py:61
  (33 shorter events, 1.7 us)
Async XLA Ops:
  7.2 184.1 %reduce-scatter.3.cloned.1.call-start = ((), (), s32[]{:S(2)}) async-start(), calls=%async_computation.3 | async-start | bytes 2654208 | tf_op jit(solution)/shard_map/reduce_scatter | solution.py:55
  7.2 10.1 %collective-permute-start = (bf16[16,4608]{1,0:T(8,128)(2,1)}, bf16[16,4608]{1,0:T(8,128)(2,1)S(1)}, u32[]{:S(2)}, u32[]{:S(2)}) collective-permute-start(bf16[16,4608]{1,0:T(8,128)(2,1)} %param.6), channel_id=1, source_target_pairs={{0,4},{4,8},{8,12},{12,16},{16,20},{20,24},{24,28},{28,0},{1,5},{5... | collective-permute-start | bytes 442376 | tf_op jit(solution)/shard_map/ppermute | solution.py:15
  17.3 7.9 %collective-permute-start.1 = (bf16[16,4608]{1,0:T(8,128)(2,1)S(1)}, bf16[16,4608]{1,0:T(8,128)(2,1)S(1)}, u32[]{:S(2)}, u32[]{:S(2)}) collective-permute-start(bf16[16,4608]{1,0:T(8,128)(2,1)S(1)} %collective-permute-done), channel_id=1, source_target_pairs={{0,4},{4,8},{8,12},{12,16},{16,20},{20,24},{24,28},{28,0},{1,5},{5... | collective-permute-start | bytes 442376 | tf_op jit(solution)/shard_map/ppermute | solution.py:15
  17.3 8.5 %collective-permute-start.4 = (bf16[16,4608]{1,0:T(8,128)(2,1)}, bf16[16,4608]{1,0:T(8,128)(2,1)S(1)}, u32[]{:S(2)}, u32[]{:S(2)}) collective-permute-start(bf16[16,4608]{1,0:T(8,128)(2,1)} %param.6), channel_id=1, source_target_pairs={{0,28},{4,0},{8,4},{12,8},{16,12},{20,16},{24,20},{28,24},{1,29},{... | collective-permute-start | bytes 442376 | tf_op jit(solution)/shard_map/ppermute | solution.py:18
  25.2 7.9 %collective-permute-start.2 = (bf16[16,4608]{1,0:T(8,128)(2,1)S(1)}, bf16[16,4608]{1,0:T(8,128)(2,1)S(1)}, u32[]{:S(2)}, u32[]{:S(2)}) collective-permute-start(bf16[16,4608]{1,0:T(8,128)(2,1)S(1)} %collective-permute-done.1), channel_id=1, source_target_pairs={{0,4},{4,8},{8,12},{12,16},{16,20},{20,24},{24,28},{28,0},{1,5},{5... | collective-permute-start | bytes 442376 | tf_op jit(solution)/shard_map/ppermute | solution.py:15
  25.8 40.4 %collective-permute-start.5 = (bf16[16,4608]{1,0:T(8,128)(2,1)S(1)}, bf16[16,4608]{1,0:T(8,128)(2,1)S(1)}, u32[]{:S(2)}, u32[]{:S(2)}) collective-permute-start(bf16[16,4608]{1,0:T(8,128)(2,1)S(1)} %collective-permute-done.4), channel_id=1, source_target_pairs={{0,28},{4,0},{8,4},{12,8},{16,12},{20,16},{24,20},{28,24},{1,29},{... | collective-permute-start | bytes 442376 | tf_op jit(solution)/shard_map/ppermute | solution.py:18
  33.2 37.7 %collective-permute-start.3 = (bf16[16,4608]{1,0:T(8,128)(2,1)S(1)}, bf16[16,4608]{1,0:T(8,128)(2,1)S(1)}, u32[]{:S(2)}, u32[]{:S(2)}) collective-permute-start(bf16[16,4608]{1,0:T(8,128)(2,1)S(1)} %collective-permute-done.2), channel_id=1, source_target_pairs={{0,4},{4,8},{8,12},{12,16},{16,20},{20,24},{24,28},{28,0},{1,5},{5... | collective-permute-start | bytes 442376 | tf_op jit(solution)/shard_map/ppermute | solution.py:15
  66.2 8.3 %copy-start = (bf16[512,4608]{1,0:T(8,128)(2,1)S(1)}, bf16[512,4608]{1,0:T(8,128)(2,1)}, u32[]{:S(2)}) copy-start(bf16[512,4608]{1,0:T(8,128)(2,1)} %param.7) | copy-start | bytes 14155780
  66.3 7.2 %collective-permute-start.6 = (bf16[16,4608]{1,0:T(8,128)(2,1)S(1)}, bf16[16,4608]{1,0:T(8,128)(2,1)S(1)}, u32[]{:S(2)}, u32[]{:S(2)}) collective-permute-start(bf16[16,4608]{1,0:T(8,128)(2,1)S(1)} %collective-permute-done.5), channel_id=1, source_target_pairs={{0,28},{4,0},{8,4},{12,8},{16,12},{20,16},{24,20},{28,24},{1,29},{... | collective-permute-start | bytes 442376 | tf_op jit(solution)/shard_map/ppermute | solution.py:18
  121.5 112.0 %all-gather.2.cloned.1.call-start = ((), (), s32[]{:S(2)}) async-start(), calls=%async_computation.2 | async-start | bytes 1327104 | tf_op jit(solution)/shard_map/all_gather | solution.py:40
  122.3 133.4 %reduce-scatter.5.cloned.1.call-start = ((), (), s32[]{:S(2)}) async-start(), calls=%async_computation.4 | async-start | bytes 368640 | tf_op jit(solution)/shard_map/reduce_scatter | solution.py:61
Sparse Core Ops, SparseCore 0:
  121.7 69.5 reduce-scatter.2
  193.4 40.0 all-gather.1
  236.6 19.0 reduce-scatter.4
